TPU v7x, 256 devices: a whole 4x4x8 slice. The times are simulated.
256 devices in a mesh: region: 8 (over x, core), dom: 32 (over z, y).
Axes of the slice: x: 4, y: 4, z: 8, core: 2. Of those that a mesh axis runs over, the one named last changes fastest.
Arguments:
- x_init: bfloat16 [1048576, 128], P(('region', 'dom')), may hold values from -6 to 6
- tiles: bfloat16 [73728, 128, 128], P(('region', 'dom'))
- tile_row: int32 [73728], P(('region', 'dom')), may hold values from 0 to 31
- tile_col: int32 [73728], P(('region', 'dom')), may hold values from 0 to 63, as said below
- send_list: int32 [256, 4, 8], P(('region', 'dom')), may hold values from 0 to 31, as said below
- send_count: int32 [256, 4], P(('region', 'dom')), may hold values from 1 to 8, as said below
Outputs:
- basis: bfloat16 [1048576, 128], P(('region', 'dom'))
- ritz_matrix: float32 [2, 128, 128], replicated
Inputs may be any that keep to these rules, and one draw needn't show every extreme that they name: `send_list`: the 8 entries of one partition and direction are distinct row tiles of that partition. `send_count`: some partition sends 8 row tiles in every direction. `tile_col`: a value 32 + d * 8 + s with d = 0 .. 3 names slot s of the d-th received stack of extended, and s is below the count that this neighbour sends; no value names a stack where the neighbour does not exist.
All inputs are finite; a program needn't handle non-finite values.
Results may differ from a plain program's by a relative error of at most 0.00115.
The roundings to bfloat16 on the way count: a program that leaves them out, or rounds other values in their place, can miss the bound.
Values may be sent and summed in bfloat16 or wider, within the bound.
No kernel may reach another device: no remote copies, remote signals or barrier semaphores. Data moves between devices by JAX's collectives and lax.ppermute only.
A program may use at most 64 MiB of HBM per device.

v0:
```python
import math
import jax
import jax.numpy as jnp
from jax import lax
from jax.sharding import PartitionSpec as P

ITERS = 2
HIGH = lax.Precision.HIGHEST


def shifted(block, axis, distance):
    devices = range(lax.axis_size(axis))
    route = [(i - distance, i) for i in devices if i - distance in devices]
    return lax.ppermute(block, axis, route)


def local_gram(current, node_total):
    return (
        lax.dot_general(
            current, current, (((0,), (0,)), ((), ())), preferred_element_type=jnp.float32
        )
        / node_total
    )


def rayleigh_sum(partial_value):
    return lax.psum(partial_value, ("region", "dom"))


def pass_dom(packed, offset):
    return shifted(packed, "dom", offset)


def pass_region(packed, offset):
    return shifted(packed, "region", offset)


def apply_graph(basis, tiles, tile_row, tile_col, send_rows, live_slot, row_tiles, tile_size):
    vectors = basis.shape[1]
    blocks = basis.reshape(row_tiles, tile_size, vectors)
    picked = blocks[send_rows]
    packed = jnp.where(live_slot[:, :, None, None], picked, jnp.zeros_like(picked))
    received = [
        pass_dom(packed[0], 1),
        pass_dom(packed[1], -1),
        pass_region(packed[2], 1),
        pass_region(packed[3], -1),
    ]
    extended = jnp.concatenate([blocks] + received, axis=0)
    group = 32
    group_count = tiles.shape[0] // group
    tile_groups = tiles.reshape(group_count, group, tile_size, tile_size)
    col_groups = tile_col.reshape(group_count, group)
    row_groups = tile_row.reshape(group_count, group)
    row_ids = jnp.arange(row_tiles, dtype=jnp.int32)

    def add_group(accumulated, pieces):
        tile_part, col_part, row_part = pieces
        gathered = extended[col_part]
        products = lax.dot_general(
            tile_part, gathered, (((2,), (1,)), ((0,), (0,))), preferred_element_type=jnp.float32
        )
        select = (row_part[None, :] == row_ids[:, None]).astype(jnp.float32)
        return (accumulated + jnp.einsum("rt,tiw->riw", select, products, precision=HIGH), None)

    start = jnp.zeros((row_tiles, tile_size, vectors), jnp.float32)
    applied, _ = lax.scan(add_group, start, (tile_groups, col_groups, row_groups))
    return applied.reshape(row_tiles * tile_size, vectors)


def shards(x_init, tiles, tile_row, tile_col, send_list, send_count):
    row_count, vectors = x_init.shape
    tile_size = tiles.shape[1]
    row_tiles = row_count // tile_size
    capacity = send_list.shape[2]
    node_total = row_count * lax.axis_size("region") * lax.axis_size("dom")
    root_total = math.sqrt(node_total)
    send_rows = send_list[0]
    live_slot = jnp.arange(capacity, dtype=jnp.int32)[None, :] < send_count[0][:, None]
    identity = jnp.eye(vectors, dtype=jnp.float32)
    current = x_init
    gram = lax.psum(local_gram(current, node_total), ("region", "dom"))
    rayleigh_list = []
    basis = x_init
    for iteration in range(ITERS):
        factor = jnp.linalg.cholesky(gram)
        inverse = lax.linalg.triangular_solve(factor, identity, left_side=True, lower=True)
        basis = jnp.dot(current.astype(jnp.float32), inverse.T, precision=HIGH).astype(jnp.bfloat16)
        applied = apply_graph(
            basis, tiles, tile_row, tile_col, send_rows, live_slot, row_tiles, tile_size
        )
        partial_value = jnp.dot(basis.astype(jnp.float32).T, applied, precision=HIGH) / root_total
        if iteration + 1 < ITERS:
            current = applied.astype(jnp.bfloat16)
            rayleigh_list.append(rayleigh_sum(partial_value))
            gram = lax.psum(local_gram(current, node_total), ("region", "dom"))
        else:
            rayleigh_list.append(rayleigh_sum(partial_value))
    return (basis, jnp.stack(rayleigh_list))


def solution(mesh):
    in_specs = (
        P(("region", "dom"), None),
        P(("region", "dom"), None, None),
        P(("region", "dom")),
        P(("region", "dom")),
        P(("region", "dom"), None, None),
        P(("region", "dom"), None),
    )
    out_specs = (P(("region", "dom"), None), P())
    return jax.shard_map(shards, mesh=mesh, in_specs=in_specs, out_specs=out_specs, check_vma=False)
```

profile of v0, /device:TPU:2, one launch (start us, length us, event | category | flops | bytes accessed | tf_op | source)
XLA Modules:
  0.0 1021.1 jit_solution(12112515196211047036)
XLA Ops:
  9.8 247.8 %all-reduce.5.cloned.1.call-done = f32[128,128]{0,1:T(8,128)} async-done(((f32[128,128]{0,1:T(8,128)}), f32[128,128]{0,1:T(8,128)}) %all-reduce.5.cloned.1.call-update) | async-done | bytes 65552 | tf_op jit(solution)/shard_map/psum | solution.py:82
  259.4 11.7 %cholesky.44 = f32[128,128]{1,0:T(8,128)S(1)} custom-call(f32[128,128]{1,0:T(8,128)S(1)} %fusion.46), custom_call_target="Cholesky" | custom-call | tf_op jit(solution)/shard_map/jit(cholesky)/cholesky | solution.py:86
  272.4 9.8 custom-call.8
  288.2 3.0 collective-permute-start
  292.6 2.4 collective-permute-start.2
  295.1 3.3 collective-permute-start.3
  298.5 3.4 collective-permute-done.1
  303.6 82.5 %while.22 = (s32[]{:T(128)}, f32[32,128,128]{2,0,1:T(8,128)}, s32[9,32]{1,0:T(8,128)S(1)}, bf16[9,32,128,128]{3,2,1,0:T(8,128)(2,1)}, s32[9,32]{1,0:T(8,128)S(1)...) while((s32[]{:T(128)}, f32[32,128,128]{2,0,1:T(8,128)}, s32[9,32]{1,0:T(8,128)S(1)}, ...), condition=%wide.region_4.7_spmd.clone, body=%wide.region_3.6_spmd.clone.sunk | while | flops 336595040 | bytes 29365292 | solution.py:67
  303.6 2.3 gather_fusion
  307.8 3.5 select_add_fusion.4
  312.8 2.3 gather_fusion
  317.0 3.5 select_add_fusion.4
  321.9 2.3 gather_fusion
  324.3 1.8 fusion.77
  326.2 3.5 select_add_fusion.4
  331.1 2.3 gather_fusion
  333.5 1.8 fusion.77
  335.4 3.5 select_add_fusion.4
  340.3 2.3 gather_fusion
  342.6 1.8 fusion.77
  344.5 3.5 select_add_fusion.4
  349.4 2.3 gather_fusion
  353.7 3.5 select_add_fusion.4
  358.6 2.3 gather_fusion
  361.0 1.8 fusion.77
  362.9 3.5 select_add_fusion.4
  367.8 2.3 gather_fusion
  372.0 3.5 select_add_fusion.4
  376.9 2.3 gather_fusion
  379.3 1.8 fusion.77
  381.2 3.5 select_add_fusion.4
  386.1 3.5 fusion.32
  389.6 2.6 copy.20
  392.2 239.2 %all-reduce.7.cloned.1.call-done = f32[128,128]{0,1:T(8,128)} async-done(((f32[128,128]{0,1:T(8,128)}), f32[128,128]{0,1:T(8,128)}) %all-reduce.7.cloned.1.call-update) | async-done | bytes 65552 | tf_op jit(solution)/shard_map/psum | solution.py:96
  633.2 11.7 %cholesky.55 = f32[128,128]{1,0:T(8,128)S(1)} custom-call(f32[128,128]{1,0:T(8,128)S(1)} %fusion.44), custom_call_target="Cholesky" | custom-call | tf_op jit(solution)/shard_map/jit(cholesky)/cholesky | solution.py:86
  646.3 9.8 custom-call.9
  656.4 2.6 convolution_convert_fusion
  661.5 4.6 collective-permute-start.4
  666.0 1.9 fusion.34
  667.9 1.9 collective-permute-start.6
  670.0 3.9 collective-permute-start.7
  675.7 1.8 collective-permute-done.7
  678.8 82.3 %while.23 = (s32[]{:T(128)}, f32[32,128,128]{2,0,1:T(8,128)}, s32[9,32]{1,0:T(8,128)S(1)}, bf16[9,32,128,128]{3,2,1,0:T(8,128)(2,1)}, s32[9,32]{1,0:T(8,128)S(1)...) while((s32[]{:T(128)}, f32[32,128,128]{2,0,1:T(8,128)}, s32[9,32]{1,0:T(8,128)S(1)}, ...), condition=%wide.region_8.11_spmd.clone, body=%wide.region_7.10_spmd.clone.sunk | while | flops 336595040 | bytes 29365292 | solution.py:67
  678.8 2.3 gather_fusion.1
  683.1 3.5 select_add_fusion.5
  688.0 2.3 gather_fusion.1
  692.2 3.5 select_add_fusion.5
  697.1 2.3 gather_fusion.1
  701.4 3.5 select_add_fusion.5
  706.3 2.3 gather_fusion.1
  710.5 3.5 select_add_fusion.5
  715.4 2.3 gather_fusion.1
  719.7 3.5 select_add_fusion.5
  724.6 2.3 gather_fusion.1
  728.8 3.5 select_add_fusion.5
  733.7 2.3 gather_fusion.1
  738.0 3.5 select_add_fusion.5
  742.9 2.3 gather_fusion.1
  747.1 3.5 select_add_fusion.5
  752.0 2.3 gather_fusion.1
  756.3 3.5 select_add_fusion.5
  761.1 2.8 copy.25
  763.9 2.0 fusion.33
  766.0 247.0 %all-reduce.9.cloned.1.call-done = (f32[1,128,128]{2,1,0:T(8,128)}, f32[1,128,128]{2,1,0:T(8,128)}) async-done(((f32[1,128,128]{2,1,0:T(8,128)}, f32[1,128,128]{2,1,0:T(8,128)}), (f32[1,128,128]{2,1,0:T(8,128)}, f32[1,128,128]{2,1,0:T(8,128)})) %all-reduce.9.cloned.1.call-update) | async-done | bytes 131088 | tf_op jit(solution)/shard_map/psum | solution.py:27
  (217 shorter events, 74.9 us)
Async XLA Ops:
  7.2 1.2 copy-start
  7.2 2.4 copy-start.15
  7.2 2.5 copy-start.14
  7.2 250.4 %all-reduce.5.cloned.1.call-start = ((), (), s32[]{:S(2)}) async-start(), calls=%async_computation | async-start | bytes 131072 | tf_op jit(solution)/shard_map/psum | solution.py:82
  9.5 621.9 %all-reduce.7.cloned.1.call-start = ((), (), s32[]{:S(2)}) async-start(), calls=%async_computation.1 | async-start | bytes 131072 | tf_op jit(solution)/shard_map/psum | solution.py:96
  283.5 2.3 copy-start.10
  285.9 6.6 copy-start.12
  285.9 6.7 copy-start.13
  288.2 10.3 %collective-permute-start = (bf16[8,128,128]{2,1,0:T(8,128)(2,1)}, bf16[8,128,128]{2,1,0:T(8,128)(2,1)S(1)}, u32[]{:S(2)}, u32[]{:S(2)}) collective-permute-start(bf16[8,128,128]{2,1,0:T(8,128)(2,1)} %get-tuple-element.159), channel_id=1, source_target_pairs={{0,1},{1,2},{2,3},{3,4},{4,5},{5,6},{6,7},{7,8},{8,9},{9,10},{10,1... | collective-permute-start | bytes 786440 | tf_op jit(solution)/shard_map/ppermute | solution.py:14
  291.2 10.8 %collective-permute-start.1 = (bf16[8,128,128]{2,1,0:T(8,128)(2,1)}, bf16[8,128,128]{2,1,0:T(8,128)(2,1)S(1)}, u32[]{:S(2)}, u32[]{:S(2)}) collective-permute-start(bf16[8,128,128]{2,1,0:T(8,128)(2,1)} %get-tuple-element.158), channel_id=1, source_target_pairs={{1,0},{2,1},{3,2},{4,3},{5,4},{6,5},{7,6},{8,7},{9,8},{10,9},{11,1... | collective-permute-start | bytes 786440 | tf_op jit(solution)/shard_map/ppermute | solution.py:14
  292.6 9.4 collective-permute-start.2
  295.1 7.0 collective-permute-start.3
  302.2 1.3 copy-start.6
  305.9 1.9 copy-start.1
  311.4 1.4 copy-start.2
  315.1 1.9 copy-start.1
  320.5 1.4 copy-start.2
  324.3 1.9 copy-start.1
  329.7 1.4 copy-start.2
  333.4 1.9 copy-start.1
  338.9 1.4 copy-start.2
  342.6 1.9 copy-start.1
  348.0 1.4 copy-start.2
  351.8 1.9 copy-start.1
  357.2 1.4 copy-start.2
  360.9 1.9 copy-start.1
  366.4 1.4 copy-start.2
  370.1 1.9 copy-start.1
  375.5 1.4 copy-start.2
  379.3 1.9 copy-start.1
  384.7 1.4 copy-start.2
  386.1 3.6 copy-start.3
  389.6 623.4 %all-reduce.9.cloned.1.call-start = ((), (), s32[]{:S(2)}) async-start(), calls=%async_computation.2 | async-start | bytes 262144 | tf_op jit(solution)/shard_map/psum | solution.py:27
  659.0 105.0 %copy-start.9 = (bf16[4096,128]{1,0:T(8,128)(2,1)}, bf16[4096,128]{1,0:T(8,128)(2,1)S(1)}, u32[]{:S(2)}) copy-start(bf16[4096,128]{1,0:T(8,128)(2,1)S(1)} %convolution_convert_fusion) | copy-start | bytes 3145732
  659.7 6.3 copy-start.8
  659.8 6.3 copy-start.11
  660.0 13.9 %collective-permute-start.5 = (bf16[8,128,128]{2,1,0:T(8,128)(2,1)S(1)}, bf16[8,128,128]{2,1,0:T(8,128)(2,1)S(1)}, u32[]{:S(2)}, u32[]{:S(2)}) collective-permute-start(bf16[8,128,128]{2,1,0:T(8,128)(2,1)S(1)} %get-tuple-element.154), channel_id=1, source_target_pairs={{1,0},{2,1},{3,2},{4,3},{5,4},{6,5},{7,6},{8,7},{9,8},{10,9},{11,1... | collective-permute-start | bytes 786440 | tf_op jit(solution)/shard_map/ppermute | solution.py:14
  661.5 12.4 %collective-permute-start.4 = (bf16[8,128,128]{2,1,0:T(8,128)(2,1)S(1)}, bf16[8,128,128]{2,1,0:T(8,128)(2,1)S(1)}, u32[]{:S(2)}, u32[]{:S(2)}) collective-permute-start(bf16[8,128,128]{2,1,0:T(8,128)(2,1)S(1)} %get-tuple-element.155), channel_id=1, source_target_pairs={{0,1},{1,2},{2,3},{3,4},{4,5},{5,6},{6,7},{7,8},{8,9},{9,10},{10,1... | collective-permute-start | bytes 786440 | tf_op jit(solution)/shard_map/ppermute | solution.py:14
  667.9 7.7 collective-permute-start.6
  670.0 7.5 collective-permute-start.7
  677.5 1.3 copy-start.7
  681.2 1.9 copy-start.4
  686.6 1.3 copy-start.5
  690.3 1.9 copy-start.4
  695.8 1.3 copy-start.5
  699.5 1.9 copy-start.4
  704.9 1.3 copy-start.5
  708.6 1.9 copy-start.4
  714.1 1.3 copy-start.5
  717.8 1.9 copy-start.4
  723.2 1.3 copy-start.5
  726.9 1.9 copy-start.4
  732.3 1.3 copy-start.5
  736.1 1.9 copy-start.4
  741.5 1.3 copy-start.5
  745.2 1.9 copy-start.4
  750.6 1.3 copy-start.5
  754.4 1.9 copy-start.4
  759.8 1.3 copy-start.5
Sparse Core Ops, SparseCore 0:
  14.1 243.4 all-reduce.4
  389.7 241.6 all-reduce.6
  766.1 246.8 all-reduce.8
where the time goes:
time: 1020 us
  waiting for transfers between devices  741 us (73%)
  matrix products  108 us (11%)
  local copies, waits for them, and re-layouts  83.8 us (8%)
  other arithmetic  50.8 us (5%)
  starting transfers between devices  21.9 us (2%)
  between operations  14.2 us (1%)
    psum x2, waiting for transfers between devices, shards(): gram = lax.psum(local_gram(current, node_total), ('region', 'dom'))  487 us
    psum x1, waiting for transfers between devices, rayleigh_sum(): return lax.psum(partial_value, ('region', 'dom'))  247 us
    dot_general x18, matrix products, add_group(): jnp.einsum('rt,tiw->riw', select, products, precision=HIGH)  63.3 us
    gather x18, local copies, waits for them, and re-layouts, add_group(): gathered = extended[col_part]  42.1 us
    dot_general x18, matrix products, add_group(): lax.dot_general(tile_part, gathered, (((2,), (1,)), ((0,), (0,))), prefer...  32.4 us
    while x72, local copies, waits for them, and re-layouts  25.8 us
    another operation x6, other arithmetic, shards(): factor = jnp.linalg.cholesky(gram)  24.8 us
    ppermute x8, starting transfers between devices, shifted(): return lax.ppermute(block, axis, route)  21.8 us
  transfers between devices with their start and end apart: 11, of which 7 were waited for; matrix products, arithmetic and copies ran while one was open for 1% of the time, Pallas kernels for 0%

commit v1 on v0

--- a/solution.py
+++ b/solution.py
@@ -93,7 +93,7 @@
         if iteration + 1 < ITERS:
             current = applied.astype(jnp.bfloat16)
             rayleigh_list.append(rayleigh_sum(partial_value))
-            gram = lax.psum(local_gram(current, node_total), ("region", "dom"))
+            gram = lax.psum(lax.psum(local_gram(current, node_total), "region"), "dom")
         else:
             rayleigh_list.append(rayleigh_sum(partial_value))
     return (basis, jnp.stack(rayleigh_list))

time: 1020 us -> 992 us (0.973)
  waiting for transfers between devices: 741 us -> 710 us
    psum x2 -> x1, waiting for transfers between devices: 487 us -> 248 us  [shards(): gram = lax.psum(local_gram(current, node_total), ('region', 'dom'))]
    psum x0 -> x2, waiting for transfers between devices: none -> 207 us  [shards(): gram = lax.psum(lax.psum(local_gram(current, node_total), 'region'), 'dom')]
  transfers between devices with their start and end apart: 11 -> 12, of which waited for: 7 -> 8; matrix products, arithmetic and copies ran while one was open for 1% -> 1% of each run, Pallas kernels for 0% -> 0%
where the time goes in v1:
time: 992 us; the launch traced here: 990 us
  waiting for transfers between devices  710 us (72%)
  matrix products  108 us (11%)
  local copies, waits for them, and re-layouts  83.8 us (8%)
  other arithmetic  50.8 us (5%)
  starting transfers between devices  21.9 us (2%)
  between operations  14.2 us (1%)
    psum x1, waiting for transfers between devices, rayleigh_sum(): return lax.psum(partial_value, ('region', 'dom'))  248 us
    psum x1, waiting for transfers between devices, shards(): gram = lax.psum(local_gram(current, node_total), ('region', 'dom'))  248 us
    psum x2, waiting for transfers between devices, shards(): gram = lax.psum(lax.psum(local_gram(current, node_total), 'region'), 'dom')  207 us
    dot_general x18, matrix products, add_group(): jnp.einsum('rt,tiw->riw', select, products, precision=HIGH)  63.3 us
    gather x18, local copies, waits for them, and re-layouts, add_group(): gathered = extended[col_part]  42.1 us
    dot_general x18, matrix products, add_group(): lax.dot_general(tile_part, gathered, (((2,), (1,)), ((0,), (0,))), prefer...  32.4 us
    while x72, local copies, waits for them, and re-layouts  25.8 us
    another operation x6, other arithmetic, shards(): factor = jnp.linalg.cholesky(gram)  24.8 us
  transfers between devices with their start and end apart: 12, of which 8 were waited for; matrix products, arithmetic and copies ran while one was open for 1% of the time, Pallas kernels for 0%

profile of v1, /device:TPU:2, one launch (start us, length us, event | category | flops | bytes accessed | tf_op | source)
XLA Modules:
  0.0 990.1 jit_solution(8419292777377338619)
XLA Ops:
  9.8 247.8 %all-reduce.6.cloned.1.call-done = f32[128,128]{0,1:T(8,128)} async-done(((f32[128,128]{0,1:T(8,128)}), f32[128,128]{0,1:T(8,128)}) %all-reduce.6.cloned.1.call-update) | async-done | bytes 65552 | tf_op jit(solution)/shard_map/psum | solution.py:82
  259.4 11.7 %cholesky.44 = f32[128,128]{1,0:T(8,128)S(1)} custom-call(f32[128,128]{1,0:T(8,128)S(1)} %fusion.46), custom_call_target="Cholesky" | custom-call | tf_op jit(solution)/shard_map/jit(cholesky)/cholesky | solution.py:86
  272.4 9.8 custom-call.8
  288.2 3.0 collective-permute-start
  292.6 2.4 collective-permute-start.2
  295.1 3.3 collective-permute-start.3
  298.5 3.4 collective-permute-done.1
  303.6 82.5 %while.22 = (s32[]{:T(128)}, f32[32,128,128]{2,0,1:T(8,128)}, s32[9,32]{1,0:T(8,128)S(1)}, bf16[9,32,128,128]{3,2,1,0:T(8,128)(2,1)}, s32[9,32]{1,0:T(8,128)S(1)...) while((s32[]{:T(128)}, f32[32,128,128]{2,0,1:T(8,128)}, s32[9,32]{1,0:T(8,128)S(1)}, ...), condition=%wide.region_4.7_spmd.clone, body=%wide.region_3.6_spmd.clone.sunk | while | flops 336595040 | bytes 29365292 | solution.py:67
  303.6 2.3 gather_fusion
  307.8 3.5 select_add_fusion.4
  312.8 2.3 gather_fusion
  317.0 3.5 select_add_fusion.4
  321.9 2.3 gather_fusion
  324.3 1.8 fusion.77
  326.2 3.5 select_add_fusion.4
  331.1 2.3 gather_fusion
  333.5 1.8 fusion.77
  335.4 3.5 select_add_fusion.4
  340.3 2.3 gather_fusion
  342.6 1.8 fusion.77
  344.5 3.5 select_add_fusion.4
  349.4 2.3 gather_fusion
  353.7 3.5 select_add_fusion.4
  358.6 2.3 gather_fusion
  362.9 3.5 select_add_fusion.4
  367.8 2.3 gather_fusion
  372.0 3.5 select_add_fusion.4
  376.9 2.3 gather_fusion
  379.3 1.8 fusion.77
  381.2 3.5 select_add_fusion.4
  386.1 3.5 fusion.32
  389.6 63.9 %all-reduce.8.cloned.1.call-done = f32[128,128]{0,1:T(8,128)} async-done(((f32[128,128]{0,1:T(8,128)}), f32[128,128]{0,1:T(8,128)}) %all-reduce.8.cloned.1.call-update) | async-done | bytes 65552 | tf_op jit(solution)/shard_map/psum | solution.py:96
  453.6 2.6 copy.20
  456.2 143.4 %all-reduce.10.cloned.1.call-done = f32[128,128]{0,1:T(8,128)} async-done(((f32[128,128]{0,1:T(8,128)}), f32[128,128]{0,1:T(8,128)}) %all-reduce.10.cloned.1.call-update) | async-done | bytes 65552 | tf_op jit(solution)/shard_map/psum | solution.py:96
  601.3 11.7 %cholesky.55 = f32[128,128]{1,0:T(8,128)S(1)} custom-call(f32[128,128]{1,0:T(8,128)S(1)} %fusion.44), custom_call_target="Cholesky" | custom-call | tf_op jit(solution)/shard_map/jit(cholesky)/cholesky | solution.py:86
  614.4 9.8 custom-call.9
  624.5 2.6 convolution_convert_fusion
  629.6 4.6 collective-permute-start.4
  634.1 1.9 fusion.34
  636.0 1.9 collective-permute-start.6
  638.1 3.9 collective-permute-start.7
  643.8 1.8 collective-permute-done.7
  646.9 82.3 %while.23 = (s32[]{:T(128)}, f32[32,128,128]{2,0,1:T(8,128)}, s32[9,32]{1,0:T(8,128)S(1)}, bf16[9,32,128,128]{3,2,1,0:T(8,128)(2,1)}, s32[9,32]{1,0:T(8,128)S(1)...) while((s32[]{:T(128)}, f32[32,128,128]{2,0,1:T(8,128)}, s32[9,32]{1,0:T(8,128)S(1)}, ...), condition=%wide.region_9.12_spmd.clone, body=%wide.region_8.11_spmd.clone.sunk | while | flops 336595040 | bytes 29365292 | solution.py:67
  646.9 2.3 gather_fusion.1
  651.2 3.5 select_add_fusion.5
  656.1 2.3 gather_fusion.1
  660.3 3.5 select_add_fusion.5
  665.2 2.3 gather_fusion.1
  669.5 3.5 select_add_fusion.5
  674.4 2.3 gather_fusion.1
  678.6 3.5 select_add_fusion.5
  683.5 2.3 gather_fusion.1
  687.8 3.5 select_add_fusion.5
  692.7 2.3 gather_fusion.1
  696.9 3.5 select_add_fusion.5
  701.8 2.3 gather_fusion.1
  706.1 3.5 select_add_fusion.5
  711.0 2.3 gather_fusion.1
  715.2 3.5 select_add_fusion.5
  720.1 2.3 gather_fusion.1
  724.4 3.5 select_add_fusion.5
  729.2 2.8 copy.25
  732.0 2.0 fusion.33
  734.1 248.0 %all-reduce.12.cloned.1.call-done = (f32[1,128,128]{2,1,0:T(8,128)}, f32[1,128,128]{2,1,0:T(8,128)}) async-done(((f32[1,128,128]{2,1,0:T(8,128)}, f32[1,128,128]{2,1,0:T(8,128)}), (f32[1,128,128]{2,1,0:T(8,128)}, f32[1,128,128]{2,1,0:T(8,128)})) %all-reduce.12.cloned.1.call-update) | async-done | bytes 131088 | tf_op jit(solution)/shard_map/psum | solution.py:27
  (220 shorter events, 76.8 us)
Async XLA Ops:
  7.2 1.2 copy-start
  7.2 2.4 copy-start.15
  7.2 2.5 copy-start.14
  7.2 250.4 %all-reduce.6.cloned.1.call-start = ((), (), s32[]{:S(2)}) async-start(), calls=%async_computation | async-start | bytes 131072 | tf_op jit(solution)/shard_map/psum | solution.py:82
  9.5 444.0 %all-reduce.8.cloned.1.call-start = ((), (), s32[]{:S(2)}) async-start(), calls=%async_computation.1 | async-start | bytes 131072 | tf_op jit(solution)/shard_map/psum | solution.py:96
  283.5 2.3 copy-start.10
  285.9 6.6 copy-start.12
  285.9 6.7 copy-start.13
  288.2 10.3 %collective-permute-start = (bf16[8,128,128]{2,1,0:T(8,128)(2,1)}, bf16[8,128,128]{2,1,0:T(8,128)(2,1)S(1)}, u32[]{:S(2)}, u32[]{:S(2)}) collective-permute-start(bf16[8,128,128]{2,1,0:T(8,128)(2,1)} %get-tuple-element.159), channel_id=1, source_target_pairs={{0,1},{1,2},{2,3},{3,4},{4,5},{5,6},{6,7},{7,8},{8,9},{9,10},{10,1... | collective-permute-start | bytes 786440 | tf_op jit(solution)/shard_map/ppermute | solution.py:14
  291.2 10.8 %collective-permute-start.1 = (bf16[8,128,128]{2,1,0:T(8,128)(2,1)}, bf16[8,128,128]{2,1,0:T(8,128)(2,1)S(1)}, u32[]{:S(2)}, u32[]{:S(2)}) collective-permute-start(bf16[8,128,128]{2,1,0:T(8,128)(2,1)} %get-tuple-element.158), channel_id=1, source_target_pairs={{1,0},{2,1},{3,2},{4,3},{5,4},{6,5},{7,6},{8,7},{9,8},{10,9},{11,1... | collective-permute-start | bytes 786440 | tf_op jit(solution)/shard_map/ppermute | solution.py:14
  292.6 9.4 collective-permute-start.2
  295.1 7.0 collective-permute-start.3
  302.2 1.3 copy-start.6
  305.9 1.9 copy-start.1
  311.4 1.4 copy-start.2
  315.1 1.9 copy-start.1
  320.5 1.4 copy-start.2
  324.3 1.9 copy-start.1
  329.7 1.4 copy-start.2
  333.4 1.9 copy-start.1
  338.9 1.4 copy-start.2
  342.6 1.9 copy-start.1
  348.0 1.4 copy-start.2
  351.8 1.9 copy-start.1
  357.2 1.4 copy-start.2
  360.9 1.9 copy-start.1
  366.4 1.4 copy-start.2
  370.1 1.9 copy-start.1
  375.5 1.4 copy-start.2
  379.3 1.9 copy-start.1
  384.7 1.4 copy-start.2
  386.1 67.5 %copy-start.3 = (f32[32,128,128]{2,0,1:T(8,128)S(1)}, f32[32,128,128]{2,0,1:T(8,128)}, u32[]{:S(2)}) copy-start(f32[32,128,128]{2,0,1:T(8,128)} %get-tuple-element.78) | copy-start | bytes 6291460
  389.6 210.0 %all-reduce.10.cloned.1.call-start = ((), (), s32[]{:S(2)}) async-start(), calls=%async_computation.2 | async-start | bytes 131072 | tf_op jit(solution)/shard_map/psum | solution.py:96
  453.5 528.6 %all-reduce.12.cloned.1.call-start = ((), (), s32[]{:S(2)}) async-start(), calls=%async_computation.3 | async-start | bytes 262144 | tf_op jit(solution)/shard_map/psum | solution.py:27
  627.1 105.0 %copy-start.9 = (bf16[4096,128]{1,0:T(8,128)(2,1)}, bf16[4096,128]{1,0:T(8,128)(2,1)S(1)}, u32[]{:S(2)}) copy-start(bf16[4096,128]{1,0:T(8,128)(2,1)S(1)} %convolution_convert_fusion) | copy-start | bytes 3145732
  627.8 6.3 copy-start.8
  627.9 6.3 copy-start.11
  628.1 13.9 %collective-permute-start.5 = (bf16[8,128,128]{2,1,0:T(8,128)(2,1)S(1)}, bf16[8,128,128]{2,1,0:T(8,128)(2,1)S(1)}, u32[]{:S(2)}, u32[]{:S(2)}) collective-permute-start(bf16[8,128,128]{2,1,0:T(8,128)(2,1)S(1)} %get-tuple-element.154), channel_id=1, source_target_pairs={{1,0},{2,1},{3,2},{4,3},{5,4},{6,5},{7,6},{8,7},{9,8},{10,9},{11,1... | collective-permute-start | bytes 786440 | tf_op jit(solution)/shard_map/ppermute | solution.py:14
  629.6 12.4 %collective-permute-start.4 = (bf16[8,128,128]{2,1,0:T(8,128)(2,1)S(1)}, bf16[8,128,128]{2,1,0:T(8,128)(2,1)S(1)}, u32[]{:S(2)}, u32[]{:S(2)}) collective-permute-start(bf16[8,128,128]{2,1,0:T(8,128)(2,1)S(1)} %get-tuple-element.155), channel_id=1, source_target_pairs={{0,1},{1,2},{2,3},{3,4},{4,5},{5,6},{6,7},{7,8},{8,9},{9,10},{10,1... | collective-permute-start | bytes 786440 | tf_op jit(solution)/shard_map/ppermute | solution.py:14
  636.0 7.7 collective-permute-start.6
  638.1 7.5 collective-permute-start.7
  645.6 1.3 copy-start.7
  649.3 1.9 copy-start.4
  654.7 1.3 copy-start.5
  658.4 1.9 copy-start.4
  663.9 1.3 copy-start.5
  667.6 1.9 copy-start.4
  673.0 1.3 copy-start.5
  676.7 1.9 copy-start.4
  682.2 1.3 copy-start.5
  685.9 1.9 copy-start.4
  691.3 1.3 copy-start.5
  695.0 1.9 copy-start.4
  700.5 1.3 copy-start.5
  704.2 1.9 copy-start.4
  709.6 1.3 copy-start.5
  713.3 1.9 copy-start.4
  718.7 1.3 copy-start.5
  722.5 1.9 copy-start.4
  727.9 1.3 copy-start.5
Sparse Core Ops, SparseCore 0:
  14.1 243.4 all-reduce.5
  389.7 63.7 all-reduce.7
  457.0 142.5 all-reduce.9
  734.2 247.8 all-reduce.11
